TPU v7x, 512 devices: a whole 4x4x16 slice. The times are simulated.
512 devices in a mesh: expert: 128 (over x, z_lo, y), dp: 4 (over z_hi, core).
Axes of the slice: x: 4, y: 4, z: 16 (z_hi: 2, z_lo: 8; z = z_hi * 8 + z_lo), core: 2. Of those that a mesh axis runs over, the one named last changes fastest.
Arguments:
- tokens: bfloat16 [8192, 2048], P(('expert', 'dp')), may hold values from -6 to 6
- cotangent: bfloat16 [8192, 2048], P(('expert', 'dp')), may hold values from -6 to 6
- route_ids: int32 [8192, 8], P(('expert', 'dp')), may hold values from 0 to 127, all different within a row; in each aligned block of 16 rows (0 to 15, 16 to 31, ...) at most 2 rows name the same one
- route_gates: bfloat16 [8192, 8], P(('expert', 'dp')), may hold values from 0.019897461 to 0.5
- gate_up: bfloat16 [128, 2048, 1536], P('expert', 'dp'), may hold values from -0.125 to 0.125
- down: bfloat16 [128, 2048, 768], P('expert', 'dp'), may hold values from -6 to 6
- moment1: bfloat16 [128, 2048, 768], P('expert', 'dp'), may hold values from -4 to 4
- moment2: bfloat16 [128, 2048, 768], P('expert', 'dp'), may hold values from 0.049804688 to 0.5
- placement: int32 [128], replicated, may hold values from 0 to 127, each once
Outputs:
- rollout_down: bfloat16 [128, 2048, 768], P('expert', None, 'dp')
Inputs may be any that keep to these rules, and one draw needn't show every extreme that they name: `route_ids`: each row names 8 different experts; within the rows of one device no expert is named more than 2 times, a bound that some block reaches. `placement`: each expert exactly once.
All inputs are finite; a program needn't handle non-finite values.
Results may differ from a plain program's by a relative error of at most 0.003.
Values may be sent and summed in bfloat16 or wider, within the bound.
A program may use at most 64 MiB of HBM per device.

v0:
```python
import jax
import jax.numpy as jnp
from jax import lax
from jax.sharding import Mesh, PartitionSpec as P

OPT_STEP = 2
BETA_ONE = 0.9
BETA_TWO = 0.95
ADAM_EPS = 1e-08
LEARN_RATE = 0.25
DP = ("zh", "core")
PLANE = ("x", "y")
EXPERT = ("x", "zl", "y")
CAP = 2
META = 128
contract_rows = (((0,), (0,)), ((), ()))


def pickers(meta, blocks, block_rows, top):
    plane = lax.axis_size(PLANE)
    wide = meta.shape[0]
    ids = meta[:, :top].astype(jnp.int32)
    gates = meta[:, top : 2 * top].astype(jnp.float32)
    place = jnp.arange(plane, dtype=jnp.int32)
    y_size = lax.axis_size("y")
    wanted = (
        place // y_size * lax.axis_size("zl") + lax.axis_index("zl")
    ) * y_size + place % y_size
    match = (ids[:, :, None] == wanted).astype(jnp.float32)
    hits = jnp.sum(match, axis=1)
    worth = jnp.sum(match * gates[:, :, None], axis=1)
    token = jnp.arange(wide, dtype=jnp.int32)
    own_block = token // block_rows
    before = (
        (own_block[:, None] == own_block[None, :]) & (token[None, :] < token[:, None])
    ).astype(jnp.bfloat16)
    earlier = jnp.dot(before, hits.astype(jnp.bfloat16), preferred_element_type=jnp.float32)
    row = jnp.arange(plane * blocks * CAP, dtype=jnp.int32)
    row_place = row // (blocks * CAP)
    spread = (row_place[:, None] == place[None, :]).astype(jnp.bfloat16)
    take = lambda v: lax.dot_general(
        spread, v.astype(jnp.bfloat16), (((1,), (1,)), ((), ())), preferred_element_type=jnp.float32
    )
    here = (row // CAP % blocks)[:, None] == own_block[None, :]
    slot = jnp.where(hits > 0, earlier, -1.0)
    chosen = here & (take(slot) == (row % CAP)[:, None].astype(jnp.float32))
    one_hot = chosen.astype(jnp.bfloat16)
    return (one_hot, jnp.where(chosen, take(worth), 0.0).astype(jnp.bfloat16))


def shards(tokens, cotangent, route_ids, route_gates, gate_up, down, moment1, moment2, placement):
    tok_rows, width = tokens.shape
    top = route_ids.shape[1]
    hidden_units = down.shape[2]
    groups = lax.axis_size(DP)
    line = lax.axis_size("zl")
    plane = lax.axis_size(PLANE)
    experts = lax.axis_size(EXPERT)
    share = width // groups
    bf16 = jnp.bfloat16
    meta = jnp.concatenate(
        [route_ids.astype(bf16), route_gates, jnp.zeros((tok_rows, META - 2 * top), bf16)], axis=1
    )
    tok_pack = lax.all_gather(jnp.concatenate([tokens, meta], axis=1), "zl", axis=0, tiled=True)
    cot_parts = cotangent.reshape(tok_rows, groups, share).transpose(1, 0, 2)
    cot_parts = jnp.concatenate(
        [cot_parts, jnp.broadcast_to(meta[None], (groups, tok_rows, META))], axis=2
    )
    cot_parts = lax.all_to_all(cot_parts, DP, split_axis=0, concat_axis=0, tiled=True)
    cot_pack = lax.all_gather(
        cot_parts.reshape(groups * tok_rows, share + META), "zl", axis=0, tiled=True
    )
    gate_up, cot_pack, tok_pack = lax.optimization_barrier((gate_up, cot_pack, tok_pack))
    weights = lax.all_gather(gate_up[0], DP, axis=0, tiled=True)
    tok_pick, _ = pickers(tok_pack[:, width:], line, tok_rows, top)
    rows = jnp.dot(tok_pick, tok_pack[:, :width], preferred_element_type=jnp.float32).astype(bf16)
    rows = lax.all_to_all(
        rows.reshape(plane, line * CAP, width), PLANE, split_axis=0, concat_axis=0, tiled=True
    ).reshape(plane * line * CAP, width)
    _, cot_pick = pickers(cot_pack[:, share:], line * groups, tok_rows, top)
    scaled = jnp.dot(cot_pick, cot_pack[:, :share], preferred_element_type=jnp.float32).astype(bf16)
    scaled = lax.all_to_all(
        scaled.reshape(plane, line * groups * CAP, share),
        PLANE,
        split_axis=0,
        concat_axis=0,
        tiled=True,
    )
    scaled = scaled.reshape(plane * line, groups, CAP, share).transpose(1, 0, 2, 3)
    scaled = scaled.reshape(groups * plane * line * CAP, share)
    pre = jnp.dot(rows, weights, preferred_element_type=jnp.float32)
    hidden = (jax.nn.silu(pre[:, :hidden_units]) * pre[:, hidden_units:]).astype(bf16)
    hidden = lax.all_gather(hidden, DP, axis=0, tiled=True)
    grad = lax.dot_general(scaled, hidden, contract_rows, preferred_element_type=jnp.float32)
    correct_one = 1.0 - BETA_ONE**OPT_STEP
    correct_two = 1.0 - BETA_TWO**OPT_STEP
    first = BETA_ONE * moment1[0].astype(jnp.float32) + (1.0 - BETA_ONE) * grad
    second = BETA_TWO * moment2[0].astype(jnp.float32) + (1.0 - BETA_TWO) * grad * grad
    direction = first / correct_one / (jnp.sqrt(second / correct_two) + ADAM_EPS)
    updated = (down[0].astype(jnp.float32) - LEARN_RATE * direction).astype(bf16)
    block_cols = hidden_units // groups
    piece_rows = share // experts
    pieces = updated.reshape(experts, piece_rows, groups, block_cols).transpose(0, 2, 1, 3)
    pieces = pieces.reshape(experts * groups, piece_rows * block_cols)
    spread = lax.all_to_all(pieces, EXPERT + DP, split_axis=0, concat_axis=0, tiled=True)
    spread = spread.reshape(experts, groups * piece_rows * block_cols)
    picked = jnp.take(spread, placement, axis=0)
    landed = lax.all_to_all(picked, EXPERT, split_axis=0, concat_axis=0, tiled=True)
    landed = landed.reshape(experts, groups, piece_rows, block_cols).transpose(1, 0, 2, 3)
    return landed.reshape(1, width, block_cols)


def solution(mesh):
    grid = Mesh(mesh.devices.reshape(4, 8, 4, 2, 2), EXPERT + DP)
    every = P(EXPERT + DP, None)
    owned = P(EXPERT, DP, None)
    placed = (every, every, every, every, owned, owned, owned, owned, P())
    return jax.shard_map(
        shards, mesh=grid, in_specs=placed, out_specs=P(EXPERT, None, DP), check_vma=False
    )
```

profile of v0, /device:TPU:1, one launch (start us, length us, event | category | flops | bytes accessed | tf_op | source)
XLA Modules:
  0.0 495.7 jit_solution(6455398087655121743)
XLA Ops:
  9.7 16.6 %all-to-all-start = ((bf16[4,16,640]{2,1,0:T(8,128)(2,1)}), bf16[4,16,640]{2,1,0:T(8,128)(2,1)S(1)}, u32[]{:S(2)}, u32[]{:S(2)}) async-start(bf16[4,16,640]{2,1,0:T(8,128)(2,1)} %copy.85), calls=%async_computation | async-start | bytes 163840 | tf_op jit(solution)/shard_map/all_to_all | solution.py:69
  26.3 0.9 concatenate.12
  27.2 42.3 %all_gather.13 = bf16[128,2176]{1,0:T(8,128)(2,1)S(1)} all-gather(bf16[16,2176]{1,0:T(8,128)(2,1)S(1)} %concatenate.12), channel_id=1, replica_groups=mesh['x'=4,'zl'=8,'y'=4,'zh'=2,'core'=2] {'zl'}, dimensions={0}, use_global_device_ids=true | all-gather | bytes 626688 | tf_op jit(solution)/shard_map/all_gather | solution.py:64
  69.5 43.4 %all_gather.12 = bf16[512,640]{1,0:T(8,128)(2,1)S(1)} all-gather(bf16[64,640]{1,0:T(8,128)(2,1)S(1)} %bitcast.41), channel_id=1, replica_groups=mesh['x'=4,'zl'=8,'y'=4,'zh'=2,'core'=2] {'zl'}, dimensions={0}, use_global_device_ids=true | all-gather | bytes 737280 | tf_op jit(solution)/shard_map/all_gather | solution.py:70
  114.3 18.3 %all_to_all.31 = bf16[16,16,2048]{2,1,0:T(8,128)(2,1)S(1)} all-to-all(bf16[16,16,2048]{2,1,0:T(8,128)(2,1)S(1)} %bitcast.36), channel_id=1, replica_groups=mesh['x'=4,'zl'=8,'y'=4,'zh'=2,'core'=2] {'x','y'}, dimensions={0} | all-to-all | bytes 2097152 | tf_op jit(solution)/shard_map/all_to_all | solution.py:77
  132.7 156.0 %all-gather.6.cloned.1.call-done = bf16[1,2048,1536]{2,1,0:T(8,128)(2,1)} async-done(((bf16[1,512,1536]{2,1,0:T(8,128)(2,1)}), bf16[1,2048,1536]{2,1,0:T(8,128)(2,1)}) %all-gather.6.cloned.1.call-update) | async-done | bytes 6291472 | tf_op jit(solution)/shard_map/all_gather | solution.py:74
  288.6 4.6 fusion
  293.2 1.0 fusion.24
  295.3 2.0 convolution_convert_fusion.1
  297.4 19.4 %all_to_all.32 = bf16[16,64,512]{2,1,0:T(8,128)(2,1)S(1)} all-to-all(bf16[16,64,512]{2,1,0:T(8,128)(2,1)} %bitcast.39), channel_id=1, replica_groups=mesh['x'=4,'zl'=8,'y'=4,'zh'=2,'core'=2] {'x','y'}, dimensions={0} | all-to-all | bytes 2097152 | tf_op jit(solution)/shard_map/all_to_all | solution.py:82
  318.3 37.2 %all-gather.4.cloned.1.call-done = bf16[1024,768]{1,0:T(8,128)(2,1)} async-done(((bf16[256,768]{1,0:T(8,128)(2,1)}), bf16[1024,768]{1,0:T(8,128)(2,1)}) %all-gather.4.cloned.1.call-update) | async-done | bytes 1572880 | tf_op jit(solution)/shard_map/all_gather | solution.py:93
  355.6 3.9 fusion.10
  359.5 0.9 reshape.257
  360.8 1.8 all_to_all.25
  363.2 5.5 %reduce.1 = bf16[512,768]{1,0:T(8,128)(2,1)S(1)} reduce(bf16[512,1,768]{2,1,0:T(2,128)(2,1)S(1)} %all_to_all.25, bf16[]{:T(256)} %broadcast.427), dimensions={1}, to_apply=%all_to_all.25.reduce_sub_computation | reduce | bytes 1572866 | tf_op jit(solution)/shard_map/all_to_all | solution.py:105
  368.7 1.1 reshape.273
  369.7 10.5 %all-to-all-start.3 = ((bf16[512,2,384]{2,1,0:T(2,128)(2,1)}), bf16[512,2,384]{2,1,0:T(2,128)(2,1)S(1)}, u32[]{:S(2)}, u32[]{:S(2)}) async-start(bf16[512,2,384]{2,1,0:T(2,128)(2,1)} %reshape.273), calls=%async_computation.3 | async-start | bytes 1572864 | tf_op jit(solution)/shard_map/all_to_all | solution.py:105
  380.2 46.2 %all-to-all-done.3 = bf16[512,2,384]{2,1,0:T(2,128)(2,1)S(1)} async-done(((bf16[512,2,384]{2,1,0:T(2,128)(2,1)}), bf16[512,2,384]{2,1,0:T(2,128)(2,1)S(1)}, u32[]{:S(2)}, u32[]{:S(2)}) %all-to-all-start.3) | async-done | bytes 786464 | tf_op jit(solution)/shard_map/all_to_all | solution.py:105
  427.1 5.0 %reduce = bf16[512,768]{1,0:T(8,128)(2,1)S(1)} reduce(bf16[512,1,768]{2,1,0:T(2,128)(2,1)S(1)} %reshape.274, bf16[]{:T(256)} %constant.215), dimensions={1}, to_apply=%all_to_all.23.reduce_sub_computation | reduce | bytes 1572866 | tf_op jit(solution)/shard_map/all_to_all | solution.py:105
  432.6 1.0 gather_fusion
  433.8 1.2 reduce.2
  435.6 48.3 %all_to_all.33 = bf16[128,2,1536]{2,1,0:T(2,128)(2,1)S(1)} all-to-all(bf16[128,2,1536]{2,1,0:T(2,128)(2,1)S(1)} %reshape.275), channel_id=1, replica_groups=mesh['x'=4,'zl'=8,'y'=4,'zh'=2,'core'=2] {'x','zl','y'}, dimensions={0} | all-to-all | bytes 1572864 | tf_op jit(solution)/shard_map/all_to_all | solution.py:108
  484.5 1.8 copy.94
  487.6 1.2 copy.96
  (49 shorter events, 12.1 us)
Async XLA Ops:
  9.7 59.8 %all-to-all-start = ((bf16[4,16,640]{2,1,0:T(8,128)(2,1)}), bf16[4,16,640]{2,1,0:T(8,128)(2,1)S(1)}, u32[]{:S(2)}, u32[]{:S(2)}) async-start(bf16[4,16,640]{2,1,0:T(8,128)(2,1)} %copy.85), calls=%async_computation | async-start | bytes 163840 | tf_op jit(solution)/shard_map/all_to_all | solution.py:69
  26.3 262.3 %all-gather.6.cloned.1.call-start = ((), (), s32[]{:S(2)}) async-start(), calls=%async_computation.6 | async-start | bytes 7864320 | tf_op jit(solution)/shard_map/all_gather | solution.py:74
  113.0 242.6 %all-gather.4.cloned.1.call-start = ((), (), s32[]{:S(2)}) async-start(), calls=%async_computation.5 | async-start | bytes 1966080 | tf_op jit(solution)/shard_map/all_gather | solution.py:93
  317.9 37.7 %copy-start = (bf16[1,512,768]{2,1,0:T(8,128)(2,1)S(1)}, bf16[1,512,768]{2,1,0:T(8,128)(2,1)}, u32[]{:S(2)}) copy-start(bf16[1,512,768]{2,1,0:T(8,128)(2,1)} %param.16) | copy-start | bytes 2359300
  368.6 11.6 %copy-start.1 = (s32[128]{0:T(128)S(1)}, s32[128]{0:T(128)}, u32[]{:S(2)}) copy-start(s32[128]{0:T(128)} %param.17) | copy-start | bytes 1540
  369.7 56.8 %all-to-all-start.3 = ((bf16[512,2,384]{2,1,0:T(2,128)(2,1)}), bf16[512,2,384]{2,1,0:T(2,128)(2,1)S(1)}, u32[]{:S(2)}, u32[]{:S(2)}) async-start(bf16[512,2,384]{2,1,0:T(2,128)(2,1)} %reshape.273), calls=%async_computation.3 | async-start | bytes 1572864 | tf_op jit(solution)/shard_map/all_to_all | solution.py:105
Sparse Core Ops, SparseCore 0:
  113.1 175.4 all-gather.5
  294.3 61.2 all-gather.3
where the time goes:
time: 496 us
  waiting for transfers between devices  239 us (48%)
  blocking collectives  172 us (35%)
  starting transfers between devices  27.1 us (5%)
  local copies, waits for them, and re-layouts  18.6 us (4%)
  between operations  13.7 us (3%)
  other arithmetic  13.2 us (3%)
  matrix products  12 us (2%)
    all_gather x1, waiting for transfers between devices, shards(): weights = lax.all_gather(gate_up[0], DP, axis=0, tiled=True)  156 us
    all_to_all x1, blocking collectives, shards(): lax.all_to_all(picked, EXPERT, split_axis=0, concat_axis=0, tiled=True)  48.3 us
    all_to_all x1, waiting for transfers between devices, shards(): lax.all_to_all(pieces, EXPERT + DP, split_axis=0, concat_axis=0, tiled=True)  46.2 us
    all_gather x1, blocking collectives, shards(): lax.all_gather(cot_parts.reshape(groups * tok_rows, share + META), 'zl',...  43.4 us
    all_gather x1, blocking collectives, shards(): lax.all_gather(jnp.concatenate([tokens, meta], axis=1), 'zl', axis=0, til...  42.3 us
    all_gather x1, waiting for transfers between devices, shards(): hidden = lax.all_gather(hidden, DP, axis=0, tiled=True)  37.2 us
    all_to_all x1, blocking collectives, shards(): lax.all_to_all(scaled.reshape(plane, line * groups * CAP, share), PLANE,...  19.4 us
    all_to_all x1, blocking collectives, shards(): lax.all_to_all(rows.reshape(plane, line * CAP, width), PLANE, split_axis=...  18.3 us
  transfers between devices with their start and end apart: 4, of which 3 were waited for; matrix products, arithmetic and copies ran while one was open for 1% of the time, Pallas kernels for 0%

commit v1 on v0

--- a/solution.py
+++ b/solution.py
@@ -61,7 +61,16 @@
     meta = jnp.concatenate(
         [route_ids.astype(bf16), route_gates, jnp.zeros((tok_rows, META - 2 * top), bf16)], axis=1
     )
-    tok_pack = lax.all_gather(jnp.concatenate([tokens, meta], axis=1), "zl", axis=0, tiled=True)
+    vec = jnp.concatenate([tokens, meta], axis=1)
+    tok_pack = jnp.concatenate(
+        lax.all_to_all(
+            jnp.stack(tuple((vec for _ in range(lax.axis_size("zl"))))),
+            axis_name="zl",
+            split_axis=0,
+            concat_axis=0,
+        ),
+        axis=0,
+    )
     cot_parts = cotangent.reshape(tok_rows, groups, share).transpose(1, 0, 2)
     cot_parts = jnp.concatenate(
         [cot_parts, jnp.broadcast_to(meta[None], (groups, tok_rows, META))], axis=2

time: 496 us -> 469 us (0.946)
  blocking collectives: 172 us -> 138 us
    all_gather x1 -> x0, blocking collectives: 42.3 us -> none  [shards(): lax.all_gather(jnp.concatenate([tokens, meta], axis=1), 'zl', axis=0, til...]
    all_to_all x1, waiting for transfers between devices: 0.01 us -> 11.1 us  [shards(): lax.all_to_all(cot_parts, DP, split_axis=0, concat_axis=0, tiled=True)]
    all_gather x1, waiting for transfers between devices: 156 us -> 146 us  [shards(): weights = lax.all_gather(gate_up[0], DP, axis=0, tiled=True)]
    all_gather x1, blocking collectives: 43.4 us -> 51.8 us  [shards(): lax.all_gather(cot_parts.reshape(groups * tok_rows, share + META), 'zl',...]
  transfers between devices with their start and end apart: 4 -> 5, of which waited for: 3 -> 4; matrix products, arithmetic and copies ran while one was open for 1% -> 1% of each run, Pallas kernels for 0% -> 0%
where the time goes in v1:
time: 469 us; the launch traced here: 468 us
  waiting for transfers between devices  241 us (51%)
  blocking collectives  138 us (29%)
  starting transfers between devices  31.9 us (7%)
  local copies, waits for them, and re-layouts  18.7 us (4%)
  between operations  13.7 us (3%)
  other arithmetic  13.6 us (3%)
  matrix products  12 us (3%)
    all_gather x1, waiting for transfers between devices, shards(): weights = lax.all_gather(gate_up[0], DP, axis=0, tiled=True)  146 us
    all_gather x1, blocking collectives, shards(): lax.all_gather(cot_parts.reshape(groups * tok_rows, share + META), 'zl',...  51.8 us
    all_to_all x1, blocking collectives, shards(): lax.all_to_all(picked, EXPERT, split_axis=0, concat_axis=0, tiled=True)  48.3 us
    all_to_all x1, waiting for transfers between devices, shards(): lax.all_to_all(pieces, EXPERT + DP, split_axis=0, concat_axis=0, tiled=True)  46.2 us
    all_gather x1, waiting for transfers between devices, shards(): hidden = lax.all_gather(hidden, DP, axis=0, tiled=True)  37.2 us
    all_to_all x1, blocking collectives, shards(): lax.all_to_all(scaled.reshape(plane, line * groups * CAP, share), PLANE,...  19.4 us
    all_to_all x1, blocking collectives, shards(): lax.all_to_all(rows.reshape(plane, line * CAP, width), PLANE, split_axis=...  18.3 us
    all_to_all x1, starting transfers between devices, shards(): lax.all_to_all(cot_parts, DP, split_axis=0, concat_axis=0, tiled=True)  16.6 us
  transfers between devices with their start and end apart: 5, of which 4 were waited for; matrix products, arithmetic and copies ran while one was open for 1% of the time, Pallas kernels for 0%

profile of v1, /device:TPU:1, one launch (start us, length us, event | category | flops | bytes accessed | tf_op | source)
XLA Modules:
  0.0 468.4 jit_solution(11811742979448897754)
XLA Ops:
  9.7 16.6 %all-to-all-start = ((bf16[4,16,640]{2,1,0:T(8,128)(2,1)}), bf16[4,16,640]{2,1,0:T(8,128)(2,1)S(1)}, u32[]{:S(2)}, u32[]{:S(2)}) async-start(bf16[4,16,640]{2,1,0:T(8,128)(2,1)} %copy.103), calls=%async_computation | async-start | bytes 163840 | tf_op jit(solution)/shard_map/all_to_all | solution.py:78
  26.3 0.9 concatenate.12
  27.2 11.1 %all-to-all-done = bf16[4,16,640]{2,1,0:T(8,128)(2,1)S(1)} async-done(((bf16[4,16,640]{2,1,0:T(8,128)(2,1)}), bf16[4,16,640]{2,1,0:T(8,128)(2,1)S(1)}, u32[]{:S(2)}, u32[]{:S(2)}) %all-to-all-start) | async-done | bytes 81952 | tf_op jit(solution)/shard_map/all_to_all | solution.py:78
  39.2 4.7 %all-to-all-start.1 = ((bf16[8,16,2176]{2,1,0:T(8,128)(2,1)}), bf16[8,16,2176]{2,1,0:T(8,128)(2,1)S(1)}, u32[]{:S(2)}, u32[]{:S(2)}) async-start(bf16[8,16,2176]{2,1,0:T(8,128)(2,1)} %stack.2), calls=%async_computation.1 | async-start | bytes 1114112 | tf_op jit(solution)/shard_map/all_to_all | solution.py:66
  44.0 51.8 %all_gather.9 = bf16[512,640]{1,0:T(8,128)(2,1)S(1)} all-gather(bf16[64,640]{1,0:T(8,128)(2,1)S(1)} %bitcast.44), channel_id=1, replica_groups=mesh['x'=4,'zl'=8,'y'=4,'zh'=2,'core'=2] {'zl'}, dimensions={0}, use_global_device_ids=true | all-gather | bytes 737280 | tf_op jit(solution)/shard_map/all_gather | solution.py:79
  97.2 18.3 %all_to_all.36 = bf16[16,16,2048]{2,1,0:T(8,128)(2,1)S(1)} all-to-all(bf16[16,16,2048]{2,1,0:T(8,128)(2,1)S(1)} %bitcast.39), channel_id=1, replica_groups=mesh['x'=4,'zl'=8,'y'=4,'zh'=2,'core'=2] {'x','y'}, dimensions={0} | all-to-all | bytes 2097152 | tf_op jit(solution)/shard_map/all_to_all | solution.py:86
  115.5 146.2 %all-gather.6.cloned.1.call-done = bf16[1,2048,1536]{2,1,0:T(8,128)(2,1)} async-done(((bf16[1,512,1536]{2,1,0:T(8,128)(2,1)}), bf16[1,2048,1536]{2,1,0:T(8,128)(2,1)}) %all-gather.6.cloned.1.call-update) | async-done | bytes 6291472 | tf_op jit(solution)/shard_map/all_gather | solution.py:83
  261.7 4.6 fusion
  266.2 1.0 fusion.24
  268.4 2.0 convolution_convert_fusion.1
  270.4 19.4 %all_to_all.37 = bf16[16,64,512]{2,1,0:T(8,128)(2,1)S(1)} all-to-all(bf16[16,64,512]{2,1,0:T(8,128)(2,1)} %bitcast.42), channel_id=1, replica_groups=mesh['x'=4,'zl'=8,'y'=4,'zh'=2,'core'=2] {'x','y'}, dimensions={0} | all-to-all | bytes 2097152 | tf_op jit(solution)/shard_map/all_to_all | solution.py:91
  291.4 37.2 %all-gather.4.cloned.1.call-done = bf16[1024,768]{1,0:T(8,128)(2,1)} async-done(((bf16[256,768]{1,0:T(8,128)(2,1)}), bf16[1024,768]{1,0:T(8,128)(2,1)}) %all-gather.4.cloned.1.call-update) | async-done | bytes 1572880 | tf_op jit(solution)/shard_map/all_gather | solution.py:102
  328.6 3.9 fusion.10
  333.9 1.8 all_to_all.29
  336.1 5.3 %reduce.1 = bf16[512,768]{1,0:T(8,128)(2,1)S(1)} reduce(bf16[512,1,768]{2,1,0:T(2,128)(2,1)S(1)} %all_to_all.29, bf16[]{:T(256)} %broadcast.429), dimensions={1}, to_apply=%all_to_all.29.reduce_sub_computation | reduce | bytes 1572866 | tf_op jit(solution)/shard_map/all_to_all | solution.py:114
  341.5 1.1 reshape.279
  342.6 10.5 %all-to-all-start.4 = ((bf16[512,2,384]{2,1,0:T(2,128)(2,1)}), bf16[512,2,384]{2,1,0:T(2,128)(2,1)S(1)}, u32[]{:S(2)}, u32[]{:S(2)}) async-start(bf16[512,2,384]{2,1,0:T(2,128)(2,1)} %reshape.279), calls=%async_computation.4 | async-start | bytes 1572864 | tf_op jit(solution)/shard_map/all_to_all | solution.py:114
  353.1 46.2 %all-to-all-done.4 = bf16[512,2,384]{2,1,0:T(2,128)(2,1)S(1)} async-done(((bf16[512,2,384]{2,1,0:T(2,128)(2,1)}), bf16[512,2,384]{2,1,0:T(2,128)(2,1)S(1)}, u32[]{:S(2)}, u32[]{:S(2)}) %all-to-all-start.4) | async-done | bytes 786464 | tf_op jit(solution)/shard_map/all_to_all | solution.py:114
  400.0 5.0 %reduce = bf16[512,768]{1,0:T(8,128)(2,1)S(1)} reduce(bf16[512,1,768]{2,1,0:T(2,128)(2,1)S(1)} %reshape.280, bf16[]{:T(256)} %constant.215), dimensions={1}, to_apply=%all_to_all.27.reduce_sub_computation | reduce | bytes 1572866 | tf_op jit(solution)/shard_map/all_to_all | solution.py:114
  405.4 1.0 gather_fusion
  406.6 1.1 reduce.2
  408.3 48.3 %all_to_all.38 = bf16[128,2,1536]{2,1,0:T(2,128)(2,1)S(1)} all-to-all(bf16[128,2,1536]{2,1,0:T(2,128)(2,1)S(1)} %reshape.281), channel_id=1, replica_groups=mesh['x'=4,'zl'=8,'y'=4,'zh'=2,'core'=2] {'x','zl','y'}, dimensions={0} | all-to-all | bytes 1572864 | tf_op jit(solution)/shard_map/all_to_all | solution.py:117
  457.2 1.8 copy.113
  460.4 1.2 copy.115
  (51 shorter events, 13.8 us)
Async XLA Ops:
  9.7 28.6 %all-to-all-start = ((bf16[4,16,640]{2,1,0:T(8,128)(2,1)}), bf16[4,16,640]{2,1,0:T(8,128)(2,1)S(1)}, u32[]{:S(2)}, u32[]{:S(2)}) async-start(bf16[4,16,640]{2,1,0:T(8,128)(2,1)} %copy.103), calls=%async_computation | async-start | bytes 163840 | tf_op jit(solution)/shard_map/all_to_all | solution.py:78
  39.2 56.6 %all-to-all-start.1 = ((bf16[8,16,2176]{2,1,0:T(8,128)(2,1)}), bf16[8,16,2176]{2,1,0:T(8,128)(2,1)S(1)}, u32[]{:S(2)}, u32[]{:S(2)}) async-start(bf16[8,16,2176]{2,1,0:T(8,128)(2,1)} %stack.2), calls=%async_computation.1 | async-start | bytes 1114112 | tf_op jit(solution)/shard_map/all_to_all | solution.py:66
  43.9 217.7 %all-gather.6.cloned.1.call-start = ((), (), s32[]{:S(2)}) async-start(), calls=%async_computation.7 | async-start | bytes 7864320 | tf_op jit(solution)/shard_map/all_gather | solution.py:83
  95.8 232.8 %all-gather.4.cloned.1.call-start = ((), (), s32[]{:S(2)}) async-start(), calls=%async_computation.6 | async-start | bytes 1966080 | tf_op jit(solution)/shard_map/all_gather | solution.py:102
  290.9 37.7 %copy-start = (bf16[1,512,768]{2,1,0:T(8,128)(2,1)S(1)}, bf16[1,512,768]{2,1,0:T(8,128)(2,1)}, u32[]{:S(2)}) copy-start(bf16[1,512,768]{2,1,0:T(8,128)(2,1)} %param.16) | copy-start | bytes 2359300
  341.5 11.6 %copy-start.1 = (s32[128]{0:T(128)S(1)}, s32[128]{0:T(128)}, u32[]{:S(2)}) copy-start(s32[128]{0:T(128)} %param.17) | copy-start | bytes 1540
  342.6 56.8 %all-to-all-start.4 = ((bf16[512,2,384]{2,1,0:T(2,128)(2,1)}), bf16[512,2,384]{2,1,0:T(2,128)(2,1)S(1)}, u32[]{:S(2)}, u32[]{:S(2)}) async-start(bf16[512,2,384]{2,1,0:T(2,128)(2,1)} %reshape.279), calls=%async_computation.4 | async-start | bytes 1572864 | tf_op jit(solution)/shard_map/all_to_all | solution.py:114
Sparse Core Ops, SparseCore 0:
  95.9 165.6 all-gather.5
  267.4 61.2 all-gather.3
